TPU v7x, 128 devices: a whole 4x4x4 slice. The times are simulated.
128 devices in a mesh: tm: 16 (over z, x), pack: 8 (over y, core).
Axes of the slice: x: 4, y: 4, z: 4, core: 2. Of those that a mesh axis runs over, the one named last changes fastest.
Arguments:
- queries: bfloat16 [8, 8192, 1024], P('pack', 'tm'), may hold values from -8 to 8
- keys: bfloat16 [8, 8192, 1024], P('pack', 'tm'), may hold values from -8 to 8
- values: bfloat16 [8, 8192, 1024], P('pack', 'tm'), may hold values from -6 to 6
- w_out: bfloat16 [1024, 1024], replicated, may hold values from -0.1875 to 0.1875
- norm_gain: float32 [1024], replicated, may hold values from 0.1 to 1.9
- block_owner: int32 [8, 64, 1], P('pack', 'tm'), may hold values from 0 to 7; in each aligned block of 4 rows (0 to 3, 4 to 7, ..., all dimensions but the last counted through in order) at most 2 rows name the same one
- block_base: int32 [8, 64], P('pack', 'tm'), may hold values from 0 to 112
- frame_offset: int32 [8, 64, 128], P('pack', 'tm'), may hold values from 0 to 15, never falling along the last dimension, each value on 1 to 16 neighbouring positions
Outputs:
- encoded: bfloat16 [8, 8192, 1024], P('pack', 'tm')
- pooled: bfloat16 [8, 2048, 1024], P('pack', 'tm')
Inputs may be any that keep to these rules, and one draw needn't show every extreme that they name: `block_owner`: among the 4 blocks of one device (aligned runs of the list), at most 2 name the same owner. `frame_offset`: within each block of 128 frames the offsets never fall and each of 0 to 15 occurs.
All inputs are finite; a program needn't handle non-finite values.
Results may differ from a plain program's by a relative error of at most 0.008.
Values may be sent and summed in bfloat16 or wider, within the bound.
A program may use at most 128 MiB of HBM per device.

v0:
```python
import jax
import jax.numpy as jnp
from jax import lax
from jax.sharding import PartitionSpec as P

HEADS = 16
LANDMARKS = 256
BLOCK = 128
POOL_DEV = 128


def mix_heads(query_rows, mark_keys, mark_values, head_count):
    row_count, model_width = query_rows.shape
    head_dim = model_width // head_count
    query_heads = query_rows.reshape(row_count, head_count, head_dim)
    key_heads = mark_keys.reshape(-1, head_count, head_dim)
    value_heads = mark_values.reshape(-1, head_count, head_dim)
    scores = jnp.einsum(
        "nhe,mhe->nhm", query_heads, key_heads, preferred_element_type=jnp.float32
    ) * head_dim ** (-0.5)
    weights = jnp.exp(scores - jnp.max(scores, axis=-1, keepdims=True))
    totals = jnp.sum(weights, axis=-1)
    blended = jnp.einsum(
        "nhm,mhe->nhe",
        weights.astype(jnp.bfloat16),
        value_heads,
        preferred_element_type=jnp.float32,
    )
    return (blended / totals[..., None]).reshape(row_count, model_width).astype(jnp.bfloat16)


def local(queries, keys, values, w_out, norm_gain, block_owner, block_base, frame_offset):
    frame_q = queries[0]
    frame_k = keys[0]
    frame_v = values[0]
    frame_count, model_width = frame_q.shape
    span = frame_count // LANDMARKS
    mark_queries = jnp.mean(
        frame_q.reshape(LANDMARKS, span, model_width), axis=1, dtype=jnp.float32
    ).astype(jnp.bfloat16)
    mark_keys = jnp.mean(
        frame_k.reshape(LANDMARKS, span, model_width), axis=1, dtype=jnp.float32
    ).astype(jnp.bfloat16)
    mark_values = mix_heads(mark_queries, frame_k, frame_v, HEADS)
    head_dim = model_width // HEADS
    query_heads = frame_q.reshape(frame_count, HEADS, head_dim)

    def absorb(running, piece_keys, piece_values):
        running_top, running_sum, running_acc = running
        key_heads = piece_keys.reshape(-1, HEADS, head_dim)
        value_heads = piece_values.reshape(-1, HEADS, head_dim)
        scores = jnp.einsum(
            "nhe,mhe->nhm", query_heads, key_heads, preferred_element_type=jnp.float32
        ) * head_dim ** (-0.5)
        new_top = jnp.maximum(running_top, jnp.max(scores, axis=-1))
        weights = jnp.exp(scores - new_top[..., None])
        rescale = jnp.exp(running_top - new_top)
        running_sum = running_sum * rescale + jnp.sum(weights, axis=-1)
        running_acc = running_acc * rescale[..., None] + jnp.einsum(
            "nhm,mhe->nhe",
            weights.astype(jnp.bfloat16),
            value_heads,
            preferred_element_type=jnp.float32,
        )
        return (new_top, running_sum, running_acc)

    start_state = (
        jnp.full((frame_count, HEADS), -1e30, jnp.float32),
        jnp.zeros((frame_count, HEADS), jnp.float32),
        jnp.zeros((frame_count, HEADS, head_dim), jnp.float32),
    )
    running = start_state
    piece_keys = lax.all_gather(mark_keys, "tm", axis=0, tiled=True)
    piece_values = lax.all_gather(mark_values, "tm", axis=0, tiled=True)
    stacked = (
        piece_keys.reshape(-1, LANDMARKS, model_width),
        piece_values.reshape(-1, LANDMARKS, model_width),
    )

    def advance(inner_state, sub_block):
        return (absorb(inner_state, sub_block[0], sub_block[1]), None)

    running, unused = lax.scan(advance, running, stacked)
    final_top, final_sum, final_acc = running
    attended = (
        (final_acc / final_sum[..., None]).reshape(frame_count, model_width).astype(jnp.bfloat16)
    )
    projected = jnp.dot(attended, w_out, preferred_element_type=jnp.float32)
    scaled = projected * lax.rsqrt(jnp.mean(projected * projected, axis=-1, keepdims=True) + 1e-06)
    encoded = (scaled * norm_gain).astype(jnp.bfloat16)
    pack_count = lax.axis_size("pack")
    owners = block_owner[0, :, 0]
    block_count = owners.shape[0]
    slot_count = max(2, 2 * block_count // pack_count)
    pack_range = jnp.arange(pack_count, dtype=jnp.int32)
    dest_hits = (owners[:, None] == pack_range[None, :]).astype(jnp.int32)
    slot_rank = jnp.sum((jnp.cumsum(dest_hits, axis=0) - dest_hits) * dest_hits, axis=1)
    chosen = (owners[None, None, :] == pack_range[:, None, None]) & (
        slot_rank[None, None, :] == jnp.arange(slot_count, dtype=jnp.int32)[None, :, None]
    )
    filled = jnp.any(chosen, axis=-1)
    source_block = jnp.sum(
        chosen.astype(jnp.int32) * jnp.arange(block_count, dtype=jnp.int32)[None, None, :], axis=-1
    )
    frame_blocks = encoded.reshape(block_count, BLOCK, model_width)
    offsets = frame_offset[0]
    block_bases = block_base[0]
    sent_rows = jnp.where(
        filled[..., None, None],
        jnp.take(frame_blocks, source_block, axis=0),
        jnp.zeros((), jnp.bfloat16),
    )
    row_targets = jnp.take(block_bases, source_block)[..., None] + jnp.take(
        offsets, source_block, axis=0
    )
    sent_targets = jnp.where(filled[..., None], row_targets, -1).astype(jnp.bfloat16)
    got_rows, got_targets = (
        lax.all_to_all(sent_rows, "pack", split_axis=0, concat_axis=0, tiled=True),
        lax.all_to_all(sent_targets, "pack", split_axis=0, concat_axis=0, tiled=True),
    )
    pool_rows = jnp.arange(POOL_DEV, dtype=jnp.int32).astype(jnp.bfloat16)
    placing = got_targets[:, :, None, :] == pool_rows[None, None, :, None]
    pool_sums = jnp.einsum(
        "scrf,scfd->rd", placing.astype(jnp.bfloat16), got_rows, preferred_element_type=jnp.float32
    )
    pool_counts = jnp.sum(placing.astype(jnp.float32), axis=(0, 1, 3))
    pooled = (pool_sums / jnp.maximum(pool_counts, 1.0)[:, None]).astype(jnp.bfloat16)
    return (encoded[None], pooled[None])


def solution(mesh):
    return jax.shard_map(
        local,
        mesh=mesh,
        in_specs=(
            P("pack", "tm", None),
            P("pack", "tm", None),
            P("pack", "tm", None),
            P(),
            P(),
            P("pack", "tm", None),
            P("pack", "tm"),
            P("pack", "tm", None),
        ),
        out_specs=(P("pack", "tm", None), P("pack", "tm", None)),
        check_vma=False,
    )
```

profile of v0, /device:TPU:1, one launch (start us, length us, event | category | flops | bytes accessed | tf_op | source)
XLA Modules:
  0.0 595.5 jit_solution(14726853507628708703)
XLA Ops:
  45.9 6.0 %all-to-all-start = ((bf16[8,2,128]{2,1,0:T(2,128)(2,1)}), bf16[8,2,128]{2,1,0:T(2,128)(2,1)S(1)}, u32[]{:S(2)}, u32[]{:S(2)}) async-start(bf16[8,2,128]{2,1,0:T(2,128)(2,1)} %select_convert_fusion), calls=%async_computation | async-start | bytes 8192 | tf_op jit(solution)/shard_map/all_to_all | solution.py:119
  53.2 54.2 %all-gather.5.cloned.1.call-done = bf16[4096,1024]{1,0:T(8,128)(2,1)} async-done(((bf16[256,1024]{1,0:T(8,128)(2,1)}), bf16[4096,1024]{1,0:T(8,128)(2,1)}) %all-gather.5.cloned.1.call-update) | async-done | bytes 8388624 | tf_op jit(solution)/shard_map/all_gather | solution.py:74
  107.4 72.6 %all-gather.3.cloned.1.call-done = bf16[4096,1024]{1,0:T(8,128)(2,1)} async-done(((bf16[256,1024]{1,0:T(8,128)(2,1)}), bf16[4096,1024]{1,0:T(8,128)(2,1)}) %all-gather.3.cloned.1.call-update) | async-done | bytes 8388624 | tf_op jit(solution)/shard_map/all_gather | solution.py:73
  180.1 338.5 %while.15 = (s32[]{:T(128)}, f32[512,16]{0,1:T(8,128)S(1)}, f32[512,16]{0,1:T(8,128)S(1)}, f32[512,16,64]{0,2,1:T(8,128)}, bf16[16,256,1024]{2,1,0:T(8,128)(2,1)...) while((s32[]{:T(128)}, f32[512,16]{0,1:T(8,128)S(1)}, ...), condition=%wide.region_7.8_spmd.clone, body=%wide.region_4.7_spmd.clone.sunk | while | flops 555261952 | bytes 36175980 | solution.py:83
  183.4 5.8 bitcast_reduce_fusion.3
  194.2 6.5 %bitcast_add_fusion.2 = f32[512,16,64]{0,2,1:T(8,128)} fusion(f32[512,16,64]{0,2,1:T(8,128)} %get-tuple-element.187, bf16[256,16,64]{0,2,1:T(8,128)(2,1)S(1)} %bitcast.93, f32[16,256,512]{2,1,0:T(8,128)} %get-tuple-element.171, f32[512,16]{0,1:T(8,128)S(1)} %select_maximum_fusion.2, f32[512,16]{0,1:T(8,128)S(1)} %get-tuple-element.174, pred[]{:T(512)S(6)} %compare.3), kind=kOutput, calls=%fused_computation.11.clone.1 | convolution fusion | flops 276299776 | bytes 13172737 | tf_op jit(solution)/shard_map/while/body/eval_jaxpr/nhm,mhe->nhe/dot_general | solution.py:59
  214.8 7.1 %bitcast_add_fusion.2 = f32[512,16,64]{0,2,1:T(8,128)} fusion(f32[512,16,64]{0,2,1:T(8,128)} %get-tuple-element.187, bf16[256,16,64]{0,2,1:T(8,128)(2,1)S(1)} %bitcast.93, f32[16,256,512]{2,1,0:T(8,128)} %get-tuple-element.171, f32[512,16]{0,1:T(8,128)S(1)} %select_maximum_fusion.2, f32[512,16]{0,1:T(8,128)S(1)} %get-tuple-element.174, pred[]{:T(512)S(6)} %compare.3), kind=kOutput, calls=%fused_computation.11.clone.1 | convolution fusion | flops 276299776 | bytes 13172737 | tf_op jit(solution)/shard_map/while/body/eval_jaxpr/nhm,mhe->nhe/dot_general | solution.py:59
  236.0 7.1 %bitcast_add_fusion.2 = f32[512,16,64]{0,2,1:T(8,128)} fusion(f32[512,16,64]{0,2,1:T(8,128)} %get-tuple-element.187, bf16[256,16,64]{0,2,1:T(8,128)(2,1)S(1)} %bitcast.93, f32[16,256,512]{2,1,0:T(8,128)} %get-tuple-element.171, f32[512,16]{0,1:T(8,128)S(1)} %select_maximum_fusion.2, f32[512,16]{0,1:T(8,128)S(1)} %get-tuple-element.174, pred[]{:T(512)S(6)} %compare.3), kind=kOutput, calls=%fused_computation.11.clone.1 | convolution fusion | flops 276299776 | bytes 13172737 | tf_op jit(solution)/shard_map/while/body/eval_jaxpr/nhm,mhe->nhe/dot_general | solution.py:59
  246.4 5.8 bitcast_reduce_fusion.3
  257.2 7.1 %bitcast_add_fusion.2 = f32[512,16,64]{0,2,1:T(8,128)} fusion(f32[512,16,64]{0,2,1:T(8,128)} %get-tuple-element.187, bf16[256,16,64]{0,2,1:T(8,128)(2,1)S(1)} %bitcast.93, f32[16,256,512]{2,1,0:T(8,128)} %get-tuple-element.171, f32[512,16]{0,1:T(8,128)S(1)} %select_maximum_fusion.2, f32[512,16]{0,1:T(8,128)S(1)} %get-tuple-element.174, pred[]{:T(512)S(6)} %compare.3), kind=kOutput, calls=%fused_computation.11.clone.1 | convolution fusion | flops 276299776 | bytes 13172737 | tf_op jit(solution)/shard_map/while/body/eval_jaxpr/nhm,mhe->nhe/dot_general | solution.py:59
  278.4 7.1 %bitcast_add_fusion.2 = f32[512,16,64]{0,2,1:T(8,128)} fusion(f32[512,16,64]{0,2,1:T(8,128)} %get-tuple-element.187, bf16[256,16,64]{0,2,1:T(8,128)(2,1)S(1)} %bitcast.93, f32[16,256,512]{2,1,0:T(8,128)} %get-tuple-element.171, f32[512,16]{0,1:T(8,128)S(1)} %select_maximum_fusion.2, f32[512,16]{0,1:T(8,128)S(1)} %get-tuple-element.174, pred[]{:T(512)S(6)} %compare.3), kind=kOutput, calls=%fused_computation.11.clone.1 | convolution fusion | flops 276299776 | bytes 13172737 | tf_op jit(solution)/shard_map/while/body/eval_jaxpr/nhm,mhe->nhe/dot_general | solution.py:59
  288.8 5.8 bitcast_reduce_fusion.3
  299.6 7.1 %bitcast_add_fusion.2 = f32[512,16,64]{0,2,1:T(8,128)} fusion(f32[512,16,64]{0,2,1:T(8,128)} %get-tuple-element.187, bf16[256,16,64]{0,2,1:T(8,128)(2,1)S(1)} %bitcast.93, f32[16,256,512]{2,1,0:T(8,128)} %get-tuple-element.171, f32[512,16]{0,1:T(8,128)S(1)} %select_maximum_fusion.2, f32[512,16]{0,1:T(8,128)S(1)} %get-tuple-element.174, pred[]{:T(512)S(6)} %compare.3), kind=kOutput, calls=%fused_computation.11.clone.1 | convolution fusion | flops 276299776 | bytes 13172737 | tf_op jit(solution)/shard_map/while/body/eval_jaxpr/nhm,mhe->nhe/dot_general | solution.py:59
  320.8 7.1 %bitcast_add_fusion.2 = f32[512,16,64]{0,2,1:T(8,128)} fusion(f32[512,16,64]{0,2,1:T(8,128)} %get-tuple-element.187, bf16[256,16,64]{0,2,1:T(8,128)(2,1)S(1)} %bitcast.93, f32[16,256,512]{2,1,0:T(8,128)} %get-tuple-element.171, f32[512,16]{0,1:T(8,128)S(1)} %select_maximum_fusion.2, f32[512,16]{0,1:T(8,128)S(1)} %get-tuple-element.174, pred[]{:T(512)S(6)} %compare.3), kind=kOutput, calls=%fused_computation.11.clone.1 | convolution fusion | flops 276299776 | bytes 13172737 | tf_op jit(solution)/shard_map/while/body/eval_jaxpr/nhm,mhe->nhe/dot_general | solution.py:59
  342.0 7.1 %bitcast_add_fusion.2 = f32[512,16,64]{0,2,1:T(8,128)} fusion(f32[512,16,64]{0,2,1:T(8,128)} %get-tuple-element.187, bf16[256,16,64]{0,2,1:T(8,128)(2,1)S(1)} %bitcast.93, f32[16,256,512]{2,1,0:T(8,128)} %get-tuple-element.171, f32[512,16]{0,1:T(8,128)S(1)} %select_maximum_fusion.2, f32[512,16]{0,1:T(8,128)S(1)} %get-tuple-element.174, pred[]{:T(512)S(6)} %compare.3), kind=kOutput, calls=%fused_computation.11.clone.1 | convolution fusion | flops 276299776 | bytes 13172737 | tf_op jit(solution)/shard_map/while/body/eval_jaxpr/nhm,mhe->nhe/dot_general | solution.py:59
  363.2 7.1 %bitcast_add_fusion.2 = f32[512,16,64]{0,2,1:T(8,128)} fusion(f32[512,16,64]{0,2,1:T(8,128)} %get-tuple-element.187, bf16[256,16,64]{0,2,1:T(8,128)(2,1)S(1)} %bitcast.93, f32[16,256,512]{2,1,0:T(8,128)} %get-tuple-element.171, f32[512,16]{0,1:T(8,128)S(1)} %select_maximum_fusion.2, f32[512,16]{0,1:T(8,128)S(1)} %get-tuple-element.174, pred[]{:T(512)S(6)} %compare.3), kind=kOutput, calls=%fused_computation.11.clone.1 | convolution fusion | flops 276299776 | bytes 13172737 | tf_op jit(solution)/shard_map/while/body/eval_jaxpr/nhm,mhe->nhe/dot_general | solution.py:59
  384.4 7.1 %bitcast_add_fusion.2 = f32[512,16,64]{0,2,1:T(8,128)} fusion(f32[512,16,64]{0,2,1:T(8,128)} %get-tuple-element.187, bf16[256,16,64]{0,2,1:T(8,128)(2,1)S(1)} %bitcast.93, f32[16,256,512]{2,1,0:T(8,128)} %get-tuple-element.171, f32[512,16]{0,1:T(8,128)S(1)} %select_maximum_fusion.2, f32[512,16]{0,1:T(8,128)S(1)} %get-tuple-element.174, pred[]{:T(512)S(6)} %compare.3), kind=kOutput, calls=%fused_computation.11.clone.1 | convolution fusion | flops 276299776 | bytes 13172737 | tf_op jit(solution)/shard_map/while/body/eval_jaxpr/nhm,mhe->nhe/dot_general | solution.py:59
  405.5 7.1 %bitcast_add_fusion.2 = f32[512,16,64]{0,2,1:T(8,128)} fusion(f32[512,16,64]{0,2,1:T(8,128)} %get-tuple-element.187, bf16[256,16,64]{0,2,1:T(8,128)(2,1)S(1)} %bitcast.93, f32[16,256,512]{2,1,0:T(8,128)} %get-tuple-element.171, f32[512,16]{0,1:T(8,128)S(1)} %select_maximum_fusion.2, f32[512,16]{0,1:T(8,128)S(1)} %get-tuple-element.174, pred[]{:T(512)S(6)} %compare.3), kind=kOutput, calls=%fused_computation.11.clone.1 | convolution fusion | flops 276299776 | bytes 13172737 | tf_op jit(solution)/shard_map/while/body/eval_jaxpr/nhm,mhe->nhe/dot_general | solution.py:59
  426.7 7.1 %bitcast_add_fusion.2 = f32[512,16,64]{0,2,1:T(8,128)} fusion(f32[512,16,64]{0,2,1:T(8,128)} %get-tuple-element.187, bf16[256,16,64]{0,2,1:T(8,128)(2,1)S(1)} %bitcast.93, f32[16,256,512]{2,1,0:T(8,128)} %get-tuple-element.171, f32[512,16]{0,1:T(8,128)S(1)} %select_maximum_fusion.2, f32[512,16]{0,1:T(8,128)S(1)} %get-tuple-element.174, pred[]{:T(512)S(6)} %compare.3), kind=kOutput, calls=%fused_computation.11.clone.1 | convolution fusion | flops 276299776 | bytes 13172737 | tf_op jit(solution)/shard_map/while/body/eval_jaxpr/nhm,mhe->nhe/dot_general | solution.py:59
  447.9 7.1 %bitcast_add_fusion.2 = f32[512,16,64]{0,2,1:T(8,128)} fusion(f32[512,16,64]{0,2,1:T(8,128)} %get-tuple-element.187, bf16[256,16,64]{0,2,1:T(8,128)(2,1)S(1)} %bitcast.93, f32[16,256,512]{2,1,0:T(8,128)} %get-tuple-element.171, f32[512,16]{0,1:T(8,128)S(1)} %select_maximum_fusion.2, f32[512,16]{0,1:T(8,128)S(1)} %get-tuple-element.174, pred[]{:T(512)S(6)} %compare.3), kind=kOutput, calls=%fused_computation.11.clone.1 | convolution fusion | flops 276299776 | bytes 13172737 | tf_op jit(solution)/shard_map/while/body/eval_jaxpr/nhm,mhe->nhe/dot_general | solution.py:59
  469.1 7.1 %bitcast_add_fusion.2 = f32[512,16,64]{0,2,1:T(8,128)} fusion(f32[512,16,64]{0,2,1:T(8,128)} %get-tuple-element.187, bf16[256,16,64]{0,2,1:T(8,128)(2,1)S(1)} %bitcast.93, f32[16,256,512]{2,1,0:T(8,128)} %get-tuple-element.171, f32[512,16]{0,1:T(8,128)S(1)} %select_maximum_fusion.2, f32[512,16]{0,1:T(8,128)S(1)} %get-tuple-element.174, pred[]{:T(512)S(6)} %compare.3), kind=kOutput, calls=%fused_computation.11.clone.1 | convolution fusion | flops 276299776 | bytes 13172737 | tf_op jit(solution)/shard_map/while/body/eval_jaxpr/nhm,mhe->nhe/dot_general | solution.py:59
  490.3 7.1 %bitcast_add_fusion.2 = f32[512,16,64]{0,2,1:T(8,128)} fusion(f32[512,16,64]{0,2,1:T(8,128)} %get-tuple-element.187, bf16[256,16,64]{0,2,1:T(8,128)(2,1)S(1)} %bitcast.93, f32[16,256,512]{2,1,0:T(8,128)} %get-tuple-element.171, f32[512,16]{0,1:T(8,128)S(1)} %select_maximum_fusion.2, f32[512,16]{0,1:T(8,128)S(1)} %get-tuple-element.174, pred[]{:T(512)S(6)} %compare.3), kind=kOutput, calls=%fused_computation.11.clone.1 | convolution fusion | flops 276299776 | bytes 13172737 | tf_op jit(solution)/shard_map/while/body/eval_jaxpr/nhm,mhe->nhe/dot_general | solution.py:59
  511.5 7.1 %bitcast_add_fusion.2 = f32[512,16,64]{0,2,1:T(8,128)} fusion(f32[512,16,64]{0,2,1:T(8,128)} %get-tuple-element.187, bf16[256,16,64]{0,2,1:T(8,128)(2,1)S(1)} %bitcast.93, f32[16,256,512]{2,1,0:T(8,128)} %get-tuple-element.171, f32[512,16]{0,1:T(8,128)S(1)} %select_maximum_fusion.2, f32[512,16]{0,1:T(8,128)S(1)} %get-tuple-element.174, pred[]{:T(512)S(6)} %compare.3), kind=kOutput, calls=%fused_computation.11.clone.1 | convolution fusion | flops 276299776 | bytes 13172737 | tf_op jit(solution)/shard_map/while/body/eval_jaxpr/nhm,mhe->nhe/dot_general | solution.py:59
  539.2 45.8 %all-to-all-done.1 = bf16[8,2,128,1024]{3,2,1,0:T(8,128)(2,1)} async-done(((bf16[8,2,128,1024]{3,2,1,0:T(8,128)(2,1)}), bf16[8,2,128,1024]{3,2,1,0:T(8,128)(2,1)}, u32[]{:S(2)}, u32[]{:S(2)}) %all-to-all-start.1) | async-done | bytes 4194336 | tf_op jit(solution)/shard_map/all_to_all | solution.py:118
  (198 shorter events, 272.6 us)
Async XLA Ops:
  7.2 513.3 %copy-start = (bf16[1024,1024]{1,0:T(8,128)(2,1)S(1)}, bf16[1024,1024]{1,0:T(8,128)(2,1)}, u32[]{:S(2)}) copy-start(bf16[1024,1024]{1,0:T(8,128)(2,1)} %param.13) | copy-start | bytes 6291460
  7.2 12.9 %copy-start.3 = (bf16[1,512,1024]{2,1,0:T(8,128)(2,1)S(1)}, bf16[1,512,1024]{2,1,0:T(8,128)(2,1)}, u32[]{:S(2)}) copy-start(bf16[1,512,1024]{2,1,0:T(8,128)(2,1)} %param.11) | copy-start | bytes 3145732
  7.2 100.3 %all-gather.5.cloned.1.call-start = ((), (), s32[]{:S(2)}) async-start(), calls=%async_computation.3 | async-start | bytes 8912896 | tf_op jit(solution)/shard_map/all_gather | solution.py:74
  26.4 1.9 copy-start.6
  33.1 9.7 %copy-start.8 = (s32[1,4,1]{1,2,0:T(1,128)S(1)}, s32[1,4,1]{1,2,0:T(1,128)}, u32[]{:S(2)}) copy-start(s32[1,4,1]{1,2,0:T(1,128)} %param.15) | copy-start | bytes 52
  33.1 10.3 %copy-start.1 = (s32[1,4]{1,0:T(1,128)S(1)}, s32[1,4]{1,0:T(1,128)}, u32[]{:S(2)}) copy-start(s32[1,4]{1,0:T(1,128)} %param.16) | copy-start | bytes 52
  33.1 146.9 %all-gather.3.cloned.1.call-start = ((), (), s32[]{:S(2)}) async-start(), calls=%async_computation.2 | async-start | bytes 8912896 | tf_op jit(solution)/shard_map/all_gather | solution.py:73
  35.5 9.2 %copy-start.5 = (s32[1,4,128]{2,1,0:T(4,128)S(1)}, s32[1,4,128]{2,1,0:T(4,128)}, u32[]{:S(2)}) copy-start(s32[1,4,128]{2,1,0:T(4,128)} %param.17) | copy-start | bytes 6148
  35.5 16.4 %copy-start.4 = (bf16[1,512,1024]{2,1,0:T(8,128)(2,1)S(1)}, bf16[1,512,1024]{2,1,0:T(8,128)(2,1)}, u32[]{:S(2)}) copy-start(bf16[1,512,1024]{2,1,0:T(8,128)(2,1)} %param.10) | copy-start | bytes 3145732
  45.9 485.1 %all-to-all-start = ((bf16[8,2,128]{2,1,0:T(2,128)(2,1)}), bf16[8,2,128]{2,1,0:T(2,128)(2,1)S(1)}, u32[]{:S(2)}, u32[]{:S(2)}) async-start(bf16[8,2,128]{2,1,0:T(2,128)(2,1)} %select_convert_fusion), calls=%async_computation | async-start | bytes 8192 | tf_op jit(solution)/shard_map/all_to_all | solution.py:119
  518.6 4.7 copy-start.7
  521.9 1.4 copy-start.2
  531.0 54.0 %all-to-all-start.1 = ((bf16[8,2,128,1024]{3,2,1,0:T(8,128)(2,1)}), bf16[8,2,128,1024]{3,2,1,0:T(8,128)(2,1)}, u32[]{:S(2)}, u32[]{:S(2)}) async-start(bf16[8,2,128,1024]{3,2,1,0:T(8,128)(2,1)} %select_select_fusion), calls=%async_computation.1 | async-start | bytes 8388608 | tf_op jit(solution)/shard_map/all_to_all | solution.py:118
Sparse Core Ops, SparseCore 0:
  33.2 74.1 all-gather.4
  109.6 70.4 all-gather.2
where the time goes:
time: 599 us; the launch traced here: 596 us
  matrix products  215 us (36%)
  waiting for transfers between devices  173 us (29%)
  other arithmetic  105 us (18%)
  local copies, waits for them, and re-layouts  77.1 us (13%)
  between operations  14.2 us (2%)
  starting transfers between devices  11.1 us (2%)
    dot_general x16, matrix products, absorb(): jnp.einsum('nhm,mhe->nhe', weights.astype(jnp.bfloat16), value_heads, pre...  113 us
    dot_general x16, matrix products, absorb(): jnp.einsum('nhe,mhe->nhm', query_heads, key_heads, preferred_element_type...  92 us
    reduce_sum x16, other arithmetic, absorb(): running_sum = running_sum * rescale + jnp.sum(weights, axis=-1)  77.1 us
    all_gather x1, waiting for transfers between devices, local(): piece_keys = lax.all_gather(mark_keys, 'tm', axis=0, tiled=True)  72.6 us
    dynamic_slice x48, local copies, waits for them, and re-layouts, local(): running, unused = lax.scan(advance, running, stacked)  56.1 us
    all_gather x1, waiting for transfers between devices, local(): piece_values = lax.all_gather(mark_values, 'tm', axis=0, tiled=True)  54.2 us
    all_to_all x1, waiting for transfers between devices, local(): lax.all_to_all(sent_rows, 'pack', split_axis=0, concat_axis=0, tiled=True)  45.8 us
  transfers between devices with their start and end apart: 4, of which 3 were waited for; matrix products, arithmetic and copies ran while one was open for 61% of the time, Pallas kernels for 0%

commit v1 on v0

--- a/solution.py
+++ b/solution.py
@@ -70,7 +70,26 @@
         jnp.zeros((frame_count, HEADS, head_dim), jnp.float32),
     )
     running = start_state
-    piece_keys = lax.all_gather(mark_keys, "tm", axis=0, tiled=True)
+    length, here, extent = (lax.axis_size("tm"), lax.axis_index("tm"), mark_keys.shape[0])
+    right = [(i, (i + 1) % length) for i in range(length)]
+    behind = [(i, (i - 1) % length) for i in range(length)]
+    filled_2 = jnp.zeros(
+        (*mark_keys.shape[:0], length * extent, *mark_keys.shape[0 + 1 :]), mark_keys.dtype
+    )
+    filled_2 = lax.dynamic_update_slice_in_dim(filled_2, mark_keys, here * extent, axis=0)
+    from_left = from_right = mark_keys
+    half = length // 2
+    for hop in range(1, half + 1):
+        from_left = lax.ppermute(from_left, "tm", right)
+        filled_2 = lax.dynamic_update_slice_in_dim(
+            filled_2, from_left, (here - hop) % length * extent, axis=0
+        )
+        if hop < length - half:
+            from_right = lax.ppermute(from_right, "tm", behind)
+            filled_2 = lax.dynamic_update_slice_in_dim(
+                filled_2, from_right, (here + hop) % length * extent, axis=0
+            )
+    piece_keys = filled_2
     piece_values = lax.all_gather(mark_values, "tm", axis=0, tiled=True)
     stacked = (
         piece_keys.reshape(-1, LANDMARKS, model_width),

time: 599 us -> 635 us (1.060)
  starting transfers between devices: 11.1 us -> 50.9 us
  waiting for transfers between devices: 173 us -> 141 us
  local copies, waits for them, and re-layouts: 77.1 us -> 107 us
    ppermute x0 -> x15, waiting for transfers between devices: none -> 95.2 us  [the longest x8 82.2 us: local(): from_left = lax.ppermute(from_left, 'tm', right)]
    all_gather x1 -> x0, waiting for transfers between devices: 72.6 us -> none  [local(): piece_keys = lax.all_gather(mark_keys, 'tm', axis=0, tiled=True)]
    all_gather x1, waiting for transfers between devices: 54.2 us -> 0.01 us  [local(): piece_values = lax.all_gather(mark_values, 'tm', axis=0, tiled=True)]
    ppermute x0 -> x15, starting transfers between devices: none -> 37.2 us  [the longest x7 35.1 us: local(): from_right = lax.ppermute(from_right, 'tm', behind)]
    dynamic_update_slice x0 -> x15, local copies, waits for them, and re-layouts: none -> 24 us  [the longest x8 13 us: local(): lax.dynamic_update_slice_in_dim(filled_2, from_left, (here - hop) % lengt...]
  transfers between devices with their start and end apart: 4 -> 18, of which waited for: 3 -> 11; matrix products, arithmetic and copies ran while one was open for 61% -> 62% of each run, Pallas kernels for 0% -> 0%
where the time goes in v1:
time: 635 us; the launch traced here: 632 us
  matrix products  214 us (34%)
  waiting for transfers between devices  141 us (22%)
  local copies, waits for them, and re-layouts  107 us (17%)
  other arithmetic  104 us (16%)
  starting transfers between devices  50.9 us (8%)
  between operations  14.2 us (2%)
    dot_general x16, matrix products, absorb(): jnp.einsum('nhm,mhe->nhe', weights.astype(jnp.bfloat16), value_heads, pre...  112 us
    dot_general x16, matrix products, absorb(): jnp.einsum('nhe,mhe->nhm', query_heads, key_heads, preferred_element_type...  91.9 us
    ppermute x8, waiting for transfers between devices, local(): from_left = lax.ppermute(from_left, 'tm', right)  82.2 us
    reduce_sum x16, other arithmetic, absorb(): running_sum = running_sum * rescale + jnp.sum(weights, axis=-1)  77.1 us
    dynamic_slice x48, local copies, waits for them, and re-layouts, local(): running, unused = lax.scan(advance, running, stacked)  56.8 us
    all_to_all x1, waiting for transfers between devices, local(): lax.all_to_all(sent_rows, 'pack', split_axis=0, concat_axis=0, tiled=True)  45.8 us
    ppermute x7, starting transfers between devices, local(): from_right = lax.ppermute(from_right, 'tm', behind)  35.1 us
    ppermute x7, waiting for transfers between devices, local(): from_right = lax.ppermute(from_right, 'tm', behind)  13 us
  transfers between devices with their start and end apart: 18, of which 11 were waited for; matrix products, arithmetic and copies ran while one was open for 62% of the time, Pallas kernels for 0%

profile of v1, /device:TPU:1, one launch (start us, length us, event | category | flops | bytes accessed | tf_op | source)
XLA Modules:
  0.0 631.5 jit_solution(5457283038239201652)
XLA Ops:
  52.6 20.0 %collective-permute-done = bf16[256,1024]{1,0:T(8,128)(2,1)S(1)} collective-permute-done((bf16[256,1024]{1,0:T(8,128)(2,1)S(1)}, bf16[256,1024]{1,0:T(8,128)(2,1)S(1)}, u32[]{:S(2)}, u32[]{:S(2)}) %collective-permute-start) | collective-permute-done | bytes 524320 | tf_op jit(solution)/shard_map/ppermute | solution.py:83
  77.3 14.7 %collective-permute-done.2 = bf16[256,1024]{1,0:T(8,128)(2,1)} collective-permute-done((bf16[256,1024]{1,0:T(8,128)(2,1)S(1)}, bf16[256,1024]{1,0:T(8,128)(2,1)}, u32[]{:S(2)}, u32[]{:S(2)}) %collective-permute-start.2) | collective-permute-done | bytes 524320 | tf_op jit(solution)/shard_map/ppermute | solution.py:83
  101.7 17.6 %collective-permute-done.4 = bf16[256,1024]{1,0:T(8,128)(2,1)} collective-permute-done((bf16[256,1024]{1,0:T(8,128)(2,1)}, bf16[256,1024]{1,0:T(8,128)(2,1)}, u32[]{:S(2)}, u32[]{:S(2)}) %collective-permute-start.4) | collective-permute-done | bytes 524320 | tf_op jit(solution)/shard_map/ppermute | solution.py:83
  128.7 15.6 %collective-permute-done.6 = bf16[256,1024]{1,0:T(8,128)(2,1)} collective-permute-done((bf16[256,1024]{1,0:T(8,128)(2,1)}, bf16[256,1024]{1,0:T(8,128)(2,1)}, u32[]{:S(2)}, u32[]{:S(2)}) %collective-permute-start.6) | collective-permute-done | bytes 524320 | tf_op jit(solution)/shard_map/ppermute | solution.py:83
  151.2 8.1 %collective-permute-done.8 = bf16[256,1024]{1,0:T(8,128)(2,1)} collective-permute-done((bf16[256,1024]{1,0:T(8,128)(2,1)}, bf16[256,1024]{1,0:T(8,128)(2,1)}, u32[]{:S(2)}, u32[]{:S(2)}) %collective-permute-start.8) | collective-permute-done | bytes 524320 | tf_op jit(solution)/shard_map/ppermute | solution.py:83
  159.9 7.2 %all-to-all-start = ((bf16[8,2,128]{2,1,0:T(2,128)(2,1)}), bf16[8,2,128]{2,1,0:T(2,128)(2,1)S(1)}, u32[]{:S(2)}, u32[]{:S(2)}) async-start(bf16[8,2,128]{2,1,0:T(2,128)(2,1)} %select_convert_fusion), calls=%async_computation | async-start | bytes 8192 | tf_op jit(solution)/shard_map/all_to_all | solution.py:138
  214.6 338.7 %while.15 = (s32[]{:T(128)}, f32[512,16]{0,1:T(8,128)S(1)}, f32[512,16]{0,1:T(8,128)S(1)}, f32[512,16,64]{0,2,1:T(8,128)}, bf16[16,256,1024]{2,1,0:T(8,128)(2,1)...) while((s32[]{:T(128)}, f32[512,16]{0,1:T(8,128)S(1)}, ...), condition=%wide.region_7.8_spmd.clone, body=%wide.region_4.7_spmd.clone.sunk | while | flops 555261952 | bytes 36175980 | solution.py:102
  228.8 6.4 %bitcast_add_fusion.2 = f32[512,16,64]{0,2,1:T(8,128)} fusion(f32[512,16,64]{0,2,1:T(8,128)} %get-tuple-element.189, bf16[256,16,64]{0,2,1:T(8,128)(2,1)S(1)} %bitcast.93, f32[16,256,512]{2,1,0:T(8,128)} %get-tuple-element.173, f32[512,16]{0,1:T(8,128)S(1)} %select_maximum_fusion.2, f32[512,16]{0,1:T(8,128)S(1)} %get-tuple-element.176, pred[]{:T(512)S(6)} %compare.18), kind=kOutput, calls=%fused_computation.11.clone.1 | convolution fusion | flops 276299776 | bytes 13172737 | tf_op jit(solution)/shard_map/while/body/eval_jaxpr/nhm,mhe->nhe/dot_general | solution.py:59
  249.4 7.0 %bitcast_add_fusion.2 = f32[512,16,64]{0,2,1:T(8,128)} fusion(f32[512,16,64]{0,2,1:T(8,128)} %get-tuple-element.189, bf16[256,16,64]{0,2,1:T(8,128)(2,1)S(1)} %bitcast.93, f32[16,256,512]{2,1,0:T(8,128)} %get-tuple-element.173, f32[512,16]{0,1:T(8,128)S(1)} %select_maximum_fusion.2, f32[512,16]{0,1:T(8,128)S(1)} %get-tuple-element.176, pred[]{:T(512)S(6)} %compare.18), kind=kOutput, calls=%fused_computation.11.clone.1 | convolution fusion | flops 276299776 | bytes 13172737 | tf_op jit(solution)/shard_map/while/body/eval_jaxpr/nhm,mhe->nhe/dot_general | solution.py:59
  270.6 7.0 %bitcast_add_fusion.2 = f32[512,16,64]{0,2,1:T(8,128)} fusion(f32[512,16,64]{0,2,1:T(8,128)} %get-tuple-element.189, bf16[256,16,64]{0,2,1:T(8,128)(2,1)S(1)} %bitcast.93, f32[16,256,512]{2,1,0:T(8,128)} %get-tuple-element.173, f32[512,16]{0,1:T(8,128)S(1)} %select_maximum_fusion.2, f32[512,16]{0,1:T(8,128)S(1)} %get-tuple-element.176, pred[]{:T(512)S(6)} %compare.18), kind=kOutput, calls=%fused_computation.11.clone.1 | convolution fusion | flops 276299776 | bytes 13172737 | tf_op jit(solution)/shard_map/while/body/eval_jaxpr/nhm,mhe->nhe/dot_general | solution.py:59
  291.8 7.0 %bitcast_add_fusion.2 = f32[512,16,64]{0,2,1:T(8,128)} fusion(f32[512,16,64]{0,2,1:T(8,128)} %get-tuple-element.189, bf16[256,16,64]{0,2,1:T(8,128)(2,1)S(1)} %bitcast.93, f32[16,256,512]{2,1,0:T(8,128)} %get-tuple-element.173, f32[512,16]{0,1:T(8,128)S(1)} %select_maximum_fusion.2, f32[512,16]{0,1:T(8,128)S(1)} %get-tuple-element.176, pred[]{:T(512)S(6)} %compare.18), kind=kOutput, calls=%fused_computation.11.clone.1 | convolution fusion | flops 276299776 | bytes 13172737 | tf_op jit(solution)/shard_map/while/body/eval_jaxpr/nhm,mhe->nhe/dot_general | solution.py:59
  313.0 7.0 %bitcast_add_fusion.2 = f32[512,16,64]{0,2,1:T(8,128)} fusion(f32[512,16,64]{0,2,1:T(8,128)} %get-tuple-element.189, bf16[256,16,64]{0,2,1:T(8,128)(2,1)S(1)} %bitcast.93, f32[16,256,512]{2,1,0:T(8,128)} %get-tuple-element.173, f32[512,16]{0,1:T(8,128)S(1)} %select_maximum_fusion.2, f32[512,16]{0,1:T(8,128)S(1)} %get-tuple-element.176, pred[]{:T(512)S(6)} %compare.18), kind=kOutput, calls=%fused_computation.11.clone.1 | convolution fusion | flops 276299776 | bytes 13172737 | tf_op jit(solution)/shard_map/while/body/eval_jaxpr/nhm,mhe->nhe/dot_general | solution.py:59
  334.2 7.0 %bitcast_add_fusion.2 = f32[512,16,64]{0,2,1:T(8,128)} fusion(f32[512,16,64]{0,2,1:T(8,128)} %get-tuple-element.189, bf16[256,16,64]{0,2,1:T(8,128)(2,1)S(1)} %bitcast.93, f32[16,256,512]{2,1,0:T(8,128)} %get-tuple-element.173, f32[512,16]{0,1:T(8,128)S(1)} %select_maximum_fusion.2, f32[512,16]{0,1:T(8,128)S(1)} %get-tuple-element.176, pred[]{:T(512)S(6)} %compare.18), kind=kOutput, calls=%fused_computation.11.clone.1 | convolution fusion | flops 276299776 | bytes 13172737 | tf_op jit(solution)/shard_map/while/body/eval_jaxpr/nhm,mhe->nhe/dot_general | solution.py:59
  355.4 7.0 %bitcast_add_fusion.2 = f32[512,16,64]{0,2,1:T(8,128)} fusion(f32[512,16,64]{0,2,1:T(8,128)} %get-tuple-element.189, bf16[256,16,64]{0,2,1:T(8,128)(2,1)S(1)} %bitcast.93, f32[16,256,512]{2,1,0:T(8,128)} %get-tuple-element.173, f32[512,16]{0,1:T(8,128)S(1)} %select_maximum_fusion.2, f32[512,16]{0,1:T(8,128)S(1)} %get-tuple-element.176, pred[]{:T(512)S(6)} %compare.18), kind=kOutput, calls=%fused_computation.11.clone.1 | convolution fusion | flops 276299776 | bytes 13172737 | tf_op jit(solution)/shard_map/while/body/eval_jaxpr/nhm,mhe->nhe/dot_general | solution.py:59
  376.6 7.0 %bitcast_add_fusion.2 = f32[512,16,64]{0,2,1:T(8,128)} fusion(f32[512,16,64]{0,2,1:T(8,128)} %get-tuple-element.189, bf16[256,16,64]{0,2,1:T(8,128)(2,1)S(1)} %bitcast.93, f32[16,256,512]{2,1,0:T(8,128)} %get-tuple-element.173, f32[512,16]{0,1:T(8,128)S(1)} %select_maximum_fusion.2, f32[512,16]{0,1:T(8,128)S(1)} %get-tuple-element.176, pred[]{:T(512)S(6)} %compare.18), kind=kOutput, calls=%fused_computation.11.clone.1 | convolution fusion | flops 276299776 | bytes 13172737 | tf_op jit(solution)/shard_map/while/body/eval_jaxpr/nhm,mhe->nhe/dot_general | solution.py:59
  397.8 7.0 %bitcast_add_fusion.2 = f32[512,16,64]{0,2,1:T(8,128)} fusion(f32[512,16,64]{0,2,1:T(8,128)} %get-tuple-element.189, bf16[256,16,64]{0,2,1:T(8,128)(2,1)S(1)} %bitcast.93, f32[16,256,512]{2,1,0:T(8,128)} %get-tuple-element.173, f32[512,16]{0,1:T(8,128)S(1)} %select_maximum_fusion.2, f32[512,16]{0,1:T(8,128)S(1)} %get-tuple-element.176, pred[]{:T(512)S(6)} %compare.18), kind=kOutput, calls=%fused_computation.11.clone.1 | convolution fusion | flops 276299776 | bytes 13172737 | tf_op jit(solution)/shard_map/while/body/eval_jaxpr/nhm,mhe->nhe/dot_general | solution.py:59
  419.0 7.0 %bitcast_add_fusion.2 = f32[512,16,64]{0,2,1:T(8,128)} fusion(f32[512,16,64]{0,2,1:T(8,128)} %get-tuple-element.189, bf16[256,16,64]{0,2,1:T(8,128)(2,1)S(1)} %bitcast.93, f32[16,256,512]{2,1,0:T(8,128)} %get-tuple-element.173, f32[512,16]{0,1:T(8,128)S(1)} %select_maximum_fusion.2, f32[512,16]{0,1:T(8,128)S(1)} %get-tuple-element.176, pred[]{:T(512)S(6)} %compare.18), kind=kOutput, calls=%fused_computation.11.clone.1 | convolution fusion | flops 276299776 | bytes 13172737 | tf_op jit(solution)/shard_map/while/body/eval_jaxpr/nhm,mhe->nhe/dot_general | solution.py:59
  440.2 7.0 %bitcast_add_fusion.2 = f32[512,16,64]{0,2,1:T(8,128)} fusion(f32[512,16,64]{0,2,1:T(8,128)} %get-tuple-element.189, bf16[256,16,64]{0,2,1:T(8,128)(2,1)S(1)} %bitcast.93, f32[16,256,512]{2,1,0:T(8,128)} %get-tuple-element.173, f32[512,16]{0,1:T(8,128)S(1)} %select_maximum_fusion.2, f32[512,16]{0,1:T(8,128)S(1)} %get-tuple-element.176, pred[]{:T(512)S(6)} %compare.18), kind=kOutput, calls=%fused_computation.11.clone.1 | convolution fusion | flops 276299776 | bytes 13172737 | tf_op jit(solution)/shard_map/while/body/eval_jaxpr/nhm,mhe->nhe/dot_general | solution.py:59
  461.4 7.0 %bitcast_add_fusion.2 = f32[512,16,64]{0,2,1:T(8,128)} fusion(f32[512,16,64]{0,2,1:T(8,128)} %get-tuple-element.189, bf16[256,16,64]{0,2,1:T(8,128)(2,1)S(1)} %bitcast.93, f32[16,256,512]{2,1,0:T(8,128)} %get-tuple-element.173, f32[512,16]{0,1:T(8,128)S(1)} %select_maximum_fusion.2, f32[512,16]{0,1:T(8,128)S(1)} %get-tuple-element.176, pred[]{:T(512)S(6)} %compare.18), kind=kOutput, calls=%fused_computation.11.clone.1 | convolution fusion | flops 276299776 | bytes 13172737 | tf_op jit(solution)/shard_map/while/body/eval_jaxpr/nhm,mhe->nhe/dot_general | solution.py:59
  482.6 7.0 %bitcast_add_fusion.2 = f32[512,16,64]{0,2,1:T(8,128)} fusion(f32[512,16,64]{0,2,1:T(8,128)} %get-tuple-element.189, bf16[256,16,64]{0,2,1:T(8,128)(2,1)S(1)} %bitcast.93, f32[16,256,512]{2,1,0:T(8,128)} %get-tuple-element.173, f32[512,16]{0,1:T(8,128)S(1)} %select_maximum_fusion.2, f32[512,16]{0,1:T(8,128)S(1)} %get-tuple-element.176, pred[]{:T(512)S(6)} %compare.18), kind=kOutput, calls=%fused_computation.11.clone.1 | convolution fusion | flops 276299776 | bytes 13172737 | tf_op jit(solution)/shard_map/while/body/eval_jaxpr/nhm,mhe->nhe/dot_general | solution.py:59
  503.8 7.0 %bitcast_add_fusion.2 = f32[512,16,64]{0,2,1:T(8,128)} fusion(f32[512,16,64]{0,2,1:T(8,128)} %get-tuple-element.189, bf16[256,16,64]{0,2,1:T(8,128)(2,1)S(1)} %bitcast.93, f32[16,256,512]{2,1,0:T(8,128)} %get-tuple-element.173, f32[512,16]{0,1:T(8,128)S(1)} %select_maximum_fusion.2, f32[512,16]{0,1:T(8,128)S(1)} %get-tuple-element.176, pred[]{:T(512)S(6)} %compare.18), kind=kOutput, calls=%fused_computation.11.clone.1 | convolution fusion | flops 276299776 | bytes 13172737 | tf_op jit(solution)/shard_map/while/body/eval_jaxpr/nhm,mhe->nhe/dot_general | solution.py:59
  525.0 7.0 %bitcast_add_fusion.2 = f32[512,16,64]{0,2,1:T(8,128)} fusion(f32[512,16,64]{0,2,1:T(8,128)} %get-tuple-element.189, bf16[256,16,64]{0,2,1:T(8,128)(2,1)S(1)} %bitcast.93, f32[16,256,512]{2,1,0:T(8,128)} %get-tuple-element.173, f32[512,16]{0,1:T(8,128)S(1)} %select_maximum_fusion.2, f32[512,16]{0,1:T(8,128)S(1)} %get-tuple-element.176, pred[]{:T(512)S(6)} %compare.18), kind=kOutput, calls=%fused_computation.11.clone.1 | convolution fusion | flops 276299776 | bytes 13172737 | tf_op jit(solution)/shard_map/while/body/eval_jaxpr/nhm,mhe->nhe/dot_general | solution.py:59
  546.2 7.0 %bitcast_add_fusion.2 = f32[512,16,64]{0,2,1:T(8,128)} fusion(f32[512,16,64]{0,2,1:T(8,128)} %get-tuple-element.189, bf16[256,16,64]{0,2,1:T(8,128)(2,1)S(1)} %bitcast.93, f32[16,256,512]{2,1,0:T(8,128)} %get-tuple-element.173, f32[512,16]{0,1:T(8,128)S(1)} %select_maximum_fusion.2, f32[512,16]{0,1:T(8,128)S(1)} %get-tuple-element.176, pred[]{:T(512)S(6)} %compare.18), kind=kOutput, calls=%fused_computation.11.clone.1 | convolution fusion | flops 276299776 | bytes 13172737 | tf_op jit(solution)/shard_map/while/body/eval_jaxpr/nhm,mhe->nhe/dot_general | solution.py:59
  575.2 45.8 %all-to-all-done.1 = bf16[8,2,128,1024]{3,2,1,0:T(8,128)(2,1)} async-done(((bf16[8,2,128,1024]{3,2,1,0:T(8,128)(2,1)}), bf16[8,2,128,1024]{3,2,1,0:T(8,128)(2,1)}, u32[]{:S(2)}, u32[]{:S(2)}) %all-to-all-start.1) | async-done | bytes 4194336 | tf_op jit(solution)/shard_map/all_to_all | solution.py:137
  (245 shorter events, 375.9 us)
Async XLA Ops:
  7.2 548.0 %copy-start = (bf16[1024,1024]{1,0:T(8,128)(2,1)S(1)}, bf16[1024,1024]{1,0:T(8,128)(2,1)}, u32[]{:S(2)}) copy-start(bf16[1024,1024]{1,0:T(8,128)(2,1)} %param.13) | copy-start | bytes 6291460
  7.2 12.8 %copy-start.3 = (bf16[1,512,1024]{2,1,0:T(8,128)(2,1)S(1)}, bf16[1,512,1024]{2,1,0:T(8,128)(2,1)}, u32[]{:S(2)}) copy-start(bf16[1,512,1024]{2,1,0:T(8,128)(2,1)} %param.11) | copy-start | bytes 3145732
  7.2 207.4 %all-gather.2.cloned.1.call-start = ((), (), s32[]{:S(2)}) async-start(), calls=%async_computation.2 | async-start | bytes 8912896 | tf_op jit(solution)/shard_map/all_gather | solution.py:93
  33.2 58.8 %copy-start.10 = (s32[1,4,1]{1,2,0:T(1,128)S(1)}, s32[1,4,1]{1,2,0:T(1,128)}, u32[]{:S(2)}) copy-start(s32[1,4,1]{1,2,0:T(1,128)} %param.15) | copy-start | bytes 52
  33.2 111.3 %copy-start.1 = (s32[1,4]{1,0:T(1,128)S(1)}, s32[1,4]{1,0:T(1,128)}, u32[]{:S(2)}) copy-start(s32[1,4]{1,0:T(1,128)} %param.16) | copy-start | bytes 52
  35.5 110.3 %copy-start.6 = (s32[1,4,128]{2,1,0:T(4,128)S(1)}, s32[1,4,128]{2,1,0:T(4,128)}, u32[]{:S(2)}) copy-start(s32[1,4,128]{2,1,0:T(4,128)} %param.17) | copy-start | bytes 6148
  40.5 126.7 %copy-start.4 = (bf16[1,512,1024]{2,1,0:T(8,128)(2,1)S(1)}, bf16[1,512,1024]{2,1,0:T(8,128)(2,1)}, u32[]{:S(2)}) copy-start(bf16[1,512,1024]{2,1,0:T(8,128)(2,1)} %param.10) | copy-start | bytes 3145732
  45.7 26.8 %collective-permute-start = (bf16[256,1024]{1,0:T(8,128)(2,1)S(1)}, bf16[256,1024]{1,0:T(8,128)(2,1)S(1)}, u32[]{:S(2)}, u32[]{:S(2)}) collective-permute-start(bf16[256,1024]{1,0:T(8,128)(2,1)S(1)} %get-tuple-element.113), channel_id=1, source_target_pairs={{0,8},{8,16},{16,24},{24,32},{32,40},{40,48},{48,56},{56,64},{64,7... | collective-permute-start | bytes 1572872 | tf_op jit(solution)/shard_map/ppermute | solution.py:83
  47.8 24.8 %collective-permute-start.1 = (bf16[256,1024]{1,0:T(8,128)(2,1)S(1)}, bf16[256,1024]{1,0:T(8,128)(2,1)}, u32[]{:S(2)}, u32[]{:S(2)}) collective-permute-start(bf16[256,1024]{1,0:T(8,128)(2,1)S(1)} %get-tuple-element.113), channel_id=1, source_target_pairs={{0,120},{8,0},{16,8},{24,16},{32,24},{40,32},{48,40},{56,48},{64,5... | collective-permute-start | bytes 1572872 | tf_op jit(solution)/shard_map/ppermute | solution.py:88
  72.5 19.4 %collective-permute-start.2 = (bf16[256,1024]{1,0:T(8,128)(2,1)S(1)}, bf16[256,1024]{1,0:T(8,128)(2,1)}, u32[]{:S(2)}, u32[]{:S(2)}) collective-permute-start(bf16[256,1024]{1,0:T(8,128)(2,1)S(1)} %collective-permute-done), channel_id=1, source_target_pairs={{0,8},{8,16},{16,24},{24,32},{32,40},{40,48},{48,56},{56,64},{64,7... | collective-permute-start | bytes 1572872 | tf_op jit(solution)/shard_map/ppermute | solution.py:83
  73.3 22.9 %collective-permute-start.3 = (bf16[256,1024]{1,0:T(8,128)(2,1)}, bf16[256,1024]{1,0:T(8,128)(2,1)}, u32[]{:S(2)}, u32[]{:S(2)}) collective-permute-start(bf16[256,1024]{1,0:T(8,128)(2,1)} %collective-permute-done.1), channel_id=1, source_target_pairs={{0,120},{8,0},{16,8},{24,16},{32,24},{40,32},{48,40},{56,48},{64,5... | collective-permute-start | bytes 1572872 | tf_op jit(solution)/shard_map/ppermute | solution.py:88
  92.0 27.3 %collective-permute-start.4 = (bf16[256,1024]{1,0:T(8,128)(2,1)}, bf16[256,1024]{1,0:T(8,128)(2,1)}, u32[]{:S(2)}, u32[]{:S(2)}) collective-permute-start(bf16[256,1024]{1,0:T(8,128)(2,1)} %collective-permute-done.2), channel_id=1, source_target_pairs={{0,8},{8,16},{16,24},{24,32},{32,40},{40,48},{48,56},{56,64},{64,7... | collective-permute-start | bytes 1572872 | tf_op jit(solution)/shard_map/ppermute | solution.py:83
  96.2 27.0 %collective-permute-start.5 = (bf16[256,1024]{1,0:T(8,128)(2,1)}, bf16[256,1024]{1,0:T(8,128)(2,1)}, u32[]{:S(2)}, u32[]{:S(2)}) collective-permute-start(bf16[256,1024]{1,0:T(8,128)(2,1)} %collective-permute-done.3), channel_id=1, source_target_pairs={{0,120},{8,0},{16,8},{24,16},{32,24},{40,32},{48,40},{56,48},{64,5... | collective-permute-start | bytes 1572872 | tf_op jit(solution)/shard_map/ppermute | solution.py:88
  119.3 25.0 %collective-permute-start.6 = (bf16[256,1024]{1,0:T(8,128)(2,1)}, bf16[256,1024]{1,0:T(8,128)(2,1)}, u32[]{:S(2)}, u32[]{:S(2)}) collective-permute-start(bf16[256,1024]{1,0:T(8,128)(2,1)} %collective-permute-done.4), channel_id=1, source_target_pairs={{0,8},{8,16},{16,24},{24,32},{32,40},{40,48},{48,56},{56,64},{64,7... | collective-permute-start | bytes 1572872 | tf_op jit(solution)/shard_map/ppermute | solution.py:83
  123.2 23.1 %collective-permute-start.7 = (bf16[256,1024]{1,0:T(8,128)(2,1)}, bf16[256,1024]{1,0:T(8,128)(2,1)}, u32[]{:S(2)}, u32[]{:S(2)}) collective-permute-start(bf16[256,1024]{1,0:T(8,128)(2,1)} %collective-permute-done.5), channel_id=1, source_target_pairs={{0,120},{8,0},{16,8},{24,16},{32,24},{40,32},{48,40},{56,48},{64,5... | collective-permute-start | bytes 1572872 | tf_op jit(solution)/shard_map/ppermute | solution.py:88
  144.3 14.9 %collective-permute-start.8 = (bf16[256,1024]{1,0:T(8,128)(2,1)}, bf16[256,1024]{1,0:T(8,128)(2,1)}, u32[]{:S(2)}, u32[]{:S(2)}) collective-permute-start(bf16[256,1024]{1,0:T(8,128)(2,1)} %collective-permute-done.6), channel_id=1, source_target_pairs={{0,8},{8,16},{16,24},{24,32},{32,40},{40,48},{48,56},{56,64},{64,7... | collective-permute-start | bytes 1572872 | tf_op jit(solution)/shard_map/ppermute | solution.py:83
  146.3 27.8 %collective-permute-start.9 = (bf16[256,1024]{1,0:T(8,128)(2,1)}, bf16[256,1024]{1,0:T(8,128)(2,1)}, u32[]{:S(2)}, u32[]{:S(2)}) collective-permute-start(bf16[256,1024]{1,0:T(8,128)(2,1)} %collective-permute-done.7), channel_id=1, source_target_pairs={{0,120},{8,0},{16,8},{24,16},{32,24},{40,32},{48,40},{56,48},{64,5... | collective-permute-start | bytes 1572872 | tf_op jit(solution)/shard_map/ppermute | solution.py:88
  159.2 21.8 %collective-permute-start.10 = (bf16[256,1024]{1,0:T(8,128)(2,1)}, bf16[256,1024]{1,0:T(8,128)(2,1)}, u32[]{:S(2)}, u32[]{:S(2)}) collective-permute-start(bf16[256,1024]{1,0:T(8,128)(2,1)} %collective-permute-done.8), channel_id=1, source_target_pairs={{0,8},{8,16},{16,24},{24,32},{32,40},{40,48},{48,56},{56,64},{64,7... | collective-permute-start | bytes 1572872 | tf_op jit(solution)/shard_map/ppermute | solution.py:83
  159.9 405.7 %all-to-all-start = ((bf16[8,2,128]{2,1,0:T(2,128)(2,1)}), bf16[8,2,128]{2,1,0:T(2,128)(2,1)S(1)}, u32[]{:S(2)}, u32[]{:S(2)}) async-start(bf16[8,2,128]{2,1,0:T(2,128)(2,1)} %select_convert_fusion), calls=%async_computation | async-start | bytes 8192 | tf_op jit(solution)/shard_map/all_to_all | solution.py:138
  174.1 16.7 %collective-permute-start.11 = (bf16[256,1024]{1,0:T(8,128)(2,1)}, bf16[256,1024]{1,0:T(8,128)(2,1)S(1)}, u32[]{:S(2)}, u32[]{:S(2)}) collective-permute-start(bf16[256,1024]{1,0:T(8,128)(2,1)} %collective-permute-done.9), channel_id=1, source_target_pairs={{0,120},{8,0},{16,8},{24,16},{32,24},{40,32},{48,40},{56,48},{64,5... | collective-permute-start | bytes 1572872 | tf_op jit(solution)/shard_map/ppermute | solution.py:88
  181.1 17.1 %collective-permute-start.12 = (bf16[256,1024]{1,0:T(8,128)(2,1)}, bf16[256,1024]{1,0:T(8,128)(2,1)S(1)}, u32[]{:S(2)}, u32[]{:S(2)}) collective-permute-start(bf16[256,1024]{1,0:T(8,128)(2,1)} %collective-permute-done.10), channel_id=1, source_target_pairs={{0,8},{8,16},{16,24},{24,32},{32,40},{40,48},{48,56},{56,64},{64,7... | collective-permute-start | bytes 1572872 | tf_op jit(solution)/shard_map/ppermute | solution.py:83
  190.8 15.9 %collective-permute-start.13 = (bf16[256,1024]{1,0:T(8,128)(2,1)S(1)}, bf16[256,1024]{1,0:T(8,128)(2,1)S(1)}, u32[]{:S(2)}, u32[]{:S(2)}) collective-permute-start(bf16[256,1024]{1,0:T(8,128)(2,1)S(1)} %collective-permute-done.11), channel_id=1, source_target_pairs={{0,120},{8,0},{16,8},{24,16},{32,24},{40,32},{48,40},{56,48},{64,5... | collective-permute-start | bytes 1572872 | tf_op jit(solution)/shard_map/ppermute | solution.py:88
  198.1 15.7 %collective-permute-start.14 = (bf16[256,1024]{1,0:T(8,128)(2,1)S(1)}, bf16[256,1024]{1,0:T(8,128)(2,1)S(1)}, u32[]{:S(2)}, u32[]{:S(2)}) collective-permute-start(bf16[256,1024]{1,0:T(8,128)(2,1)S(1)} %collective-permute-done.12), channel_id=1, source_target_pairs={{0,8},{8,16},{16,24},{24,32},{32,40},{40,48},{48,56},{56,64},{64,7... | collective-permute-start | bytes 1572872 | tf_op jit(solution)/shard_map/ppermute | solution.py:83
  565.6 55.4 %all-to-all-start.1 = ((bf16[8,2,128,1024]{3,2,1,0:T(8,128)(2,1)}), bf16[8,2,128,1024]{3,2,1,0:T(8,128)(2,1)}, u32[]{:S(2)}, u32[]{:S(2)}) async-start(bf16[8,2,128,1024]{3,2,1,0:T(8,128)(2,1)} %select_select_fusion), calls=%async_computation.1 | async-start | bytes 8388608 | tf_op jit(solution)/shard_map/all_to_all | solution.py:137
  (5 other events, 15.9 us)
Sparse Core Ops, SparseCore 0:
  33.3 109.3 all-gather.1
